TPU v7x, 32 devices: a whole 2x2x4 slice. The times are simulated.
32 devices in a mesh: freq: 2 (over x), src: 16 (over z, y, core).
Axes of the slice: x: 2, y: 2, z: 4, core: 2. Of those that a mesh axis runs over, the one named last changes fastest.
Arguments:
- shots: bfloat16 [4, 8192, 8192], P('freq', 'src'), parts along dimension 0, may hold values from -6 to 6
- wavelet: float32 [4, 8192], P('freq', 'src'), parts along dimension 0, may hold values from -1.2 to 1.2
- obliquity: float32 [8192], P('src'), may hold values from 0.3 to 3
- aperture: int32 [64, 64, 4], P('src'), may hold values from -1 to 63, as said below
Outputs:
- multiples: bfloat16 [4, 8192, 8192], P('freq', None, 'src'), parts along dimension 0
There are 2 independent parts, one for each index of `freq`. A program takes and returns all parts, laid end to end along the dimension named above; an argument that names none is the same for every part. Nothing has to cross between parts.
Inputs may be any that keep to these rules, and one draw needn't show every extreme that they name: `aperture`: entry (i, j, t) is -1 (unused) or a block k with |k - j| <= 2; no block stands twice in one list.
All inputs are finite; a program needn't handle non-finite values.
Results may differ from a plain program's by a relative error of at most 0.0072.
Values may be sent and summed in bfloat16 or wider, within the bound.
A program may use at most 192 MiB of HBM per device.

v0:
```python
import jax
import jax.numpy as jnp
from jax import lax
from jax.sharding import PartitionSpec as P

BLK = 128
APW = 2


def block_column(lefts, rights, mask_col, row_count):
    row_blocks = row_count // BLK
    window_len = len(lefts)
    left_all = jnp.stack(lefts, axis=2).reshape(2, row_blocks, BLK, window_len, BLK)
    left_all = left_all * mask_col.astype(jnp.bfloat16)[None, :, None, :, None]
    left_all = left_all.reshape(2, row_count, window_len * BLK)
    left_big = jnp.concatenate([left_all[0], left_all[1]], axis=1)
    right_re = jnp.concatenate([r[0] for r in rights], axis=0)
    right_im = jnp.concatenate([r[1] for r in rights], axis=0)
    right_big = jnp.concatenate(
        [
            jnp.concatenate([right_re, right_im], axis=1),
            jnp.concatenate([-right_im, right_re], axis=1),
        ],
        axis=0,
    )
    product = jnp.dot(left_big, right_big, preferred_element_type=jnp.float32)
    return -jnp.stack([product[:, :BLK], product[:, BLK:]])


def valid_targets(targets, block_total):
    return jnp.where((targets >= 0) & (targets < block_total), targets, -2)


def per_device(shots, wavelet, obliquity, aperture):
    shot_re = shots[0].astype(jnp.float32)
    shot_im = shots[1].astype(jnp.float32)
    wave_re = wavelet[0][:, None]
    wave_im = wavelet[1][:, None]
    scaled = jnp.stack(
        [shot_re * wave_re - shot_im * wave_im, shot_re * wave_im + shot_im * wave_re]
    ).astype(jnp.bfloat16)
    window_len = 2 * APW + 1
    offsets = jnp.arange(window_len, dtype=jnp.int32) - APW
    scales = lax.all_gather(obliquity, "src", axis=0, tiled=True)
    data = (scaled.astype(jnp.float32) * scales).astype(jnp.bfloat16)
    row_count = data.shape[1]
    row_blocks = row_count // BLK
    block_count = data.shape[2] // BLK
    base_block = lax.axis_index("src") * row_blocks
    band_rows = []
    for r in range(row_blocks):
        row_pieces = []
        for u in range(window_len):
            c_block = jnp.clip(base_block + r + u - APW, 0, block_count - 1)
            row_pieces.append(
                lax.dynamic_slice(
                    data, (jnp.int32(0), jnp.int32(r * BLK), c_block * BLK), (2, BLK, BLK)
                )
            )
        band_rows.append(jnp.stack(row_pieces))
    band_local = jnp.stack(band_rows)
    band_all = lax.all_gather(band_local, "src", axis=0, tiled=True)
    column_ids = jnp.arange(block_count, dtype=jnp.int32)
    targets_all = valid_targets(column_ids[:, None] + offsets[None, :], block_count)
    mask_all = jnp.any(aperture[:, :, :, None] == targets_all[None, :, None, :], axis=2)

    def one_group(g, output):
        for u in range(8):
            j = g * 8 + u
            mask_col = lax.dynamic_index_in_dim(mask_all, j, 1, keepdims=False)
            lefts = []
            rights = []
            for w in range(window_len):
                k_block = jnp.clip(j + w - APW, 0, block_count - 1)
                lefts.append(
                    lax.dynamic_slice(
                        data, (jnp.int32(0), jnp.int32(0), k_block * BLK), (2, row_count, BLK)
                    )
                )
                rights.append(
                    lax.dynamic_index_in_dim(
                        lax.dynamic_index_in_dim(band_all, k_block, 0, keepdims=False),
                        2 * APW - w,
                        0,
                        keepdims=False,
                    )
                )
            column = block_column(lefts, rights, mask_col, row_count).astype(jnp.bfloat16)
            output = lax.dynamic_update_slice(output, column, (jnp.int32(0), jnp.int32(0), j * BLK))
        return output

    rows_result = lax.fori_loop(
        0, block_count // 8, one_group, jnp.zeros((2, row_count, block_count * BLK), jnp.bfloat16)
    )
    return lax.all_to_all(rows_result, "src", split_axis=2, concat_axis=1, tiled=True)


def solution(mesh):
    return jax.shard_map(
        per_device,
        mesh=mesh,
        in_specs=(P("freq", "src", None), P("freq", "src"), P("src"), P("src", None, None)),
        out_specs=P("freq", None, "src"),
        check_vma=False,
    )
```

profile of v0, /device:TPU:1, one launch (start us, length us, event | category | flops | bytes accessed | tf_op | source)
XLA Modules:
  0.0 1068.1 jit_solution(2346869558573901106)
XLA Ops:
  7.3 23.3 %all-gather = f32[16,1,512]{2,1,0:T(1,128)S(1)} all-gather(f32[1,1,512]{2,1,0:T(1,128)} %bitcast.648), channel_id=1, replica_groups=mesh['freq'=2,'src'=16] {'src'}, dimensions={0}, use_global_device_ids=true | all-gather | bytes 34816 | tf_op jit(solution)/shard_map/all_gather | solution.py:44
  30.6 11.8 %fusion.144 = (bf16[1,512,8192]{2,1,0:T(8,128)(2,1)}, bf16[1,512,8192]{2,1,0:T(8,128)(2,1)}) fusion(bf16[2,512,8192]{2,1,0:T(8,128)(2,1)} %param.6), kind=kLoop, calls=%fused_computation.461 | loop fusion | bytes 33554432 | tf_op jit(solution)/shard_map/slice | solution.py:36
  42.4 11.9 %copy.114 = bf16[1,512,8192]{1,2,0:T(8,128)(2,1)} copy(bf16[1,512,8192]{2,1,0:T(8,128)(2,1)} %get-tuple-element.547) | data formatting | bytes 16777216
  54.3 11.9 %copy.113 = bf16[1,512,8192]{1,2,0:T(8,128)(2,1)} copy(bf16[1,512,8192]{2,1,0:T(8,128)(2,1)} %get-tuple-element.548) | data formatting | bytes 16777216
  66.2 8.8 fusion.129
  75.0 3.3 multiply_convert_fusion
  78.3 5.8 copy-done
  87.5 1.2 pad_maximum_fusion
  89.6 105.3 %all-gather.3.cloned.1.call-done = bf16[64,5,2,128,128]{4,3,2,1,0:T(8,128)(2,1)} async-done(((bf16[4,5,2,128,128]{4,3,2,1,0:T(8,128)(2,1)}), bf16[64,5,2,128,128]{4,3,2,1,0:T(8,128)(2,1)}) %all-gather.3.cloned.1.call-update) | async-done | bytes 20971536 | tf_op jit(solution)/shard_map/all_gather | solution.py:62
  194.9 6.1 broadcast_in_dim.36
  201.0 410.3 %while.18 = (s32[]{:T(128)}, bf16[2,512,8192]{2,1,0:T(8,128)(2,1)}, bf16[2,512,8192]{1,2,0:T(8,128)(2,1)}, pred[4,64,5]{2,0,1:T(4,128)(4,1)S(1)}, bf16[64,5,2,12...) while((s32[]{:T(128)}, bf16[2,512,8192]{2,1,0:T(8,128)(2,1)}, ...), condition=%wide.region_2.3_spmd, body=%wide.region_1.2_spmd.sunk | while | flops 2735341824 | bytes 156504944 | solution.py:92
  204.5 0.9 constant_dynamic-update-slice_fusion.149
  205.3 1.2 constant_dynamic-update-slice_fusion.150
  208.1 1.0 constant_dynamic-update-slice_fusion.153
  209.1 1.0 constant_dynamic-update-slice_fusion.154
  210.2 1.1 constant_dynamic-update-slice_fusion.155
  211.3 1.0 constant_dynamic-update-slice_fusion.156
  216.9 2.1 constant_dynamic-slice_fusion.41
  255.7 0.9 constant_dynamic-update-slice_fusion.149
  256.6 1.2 constant_dynamic-update-slice_fusion.150
  259.4 1.0 constant_dynamic-update-slice_fusion.153
  260.4 1.0 constant_dynamic-update-slice_fusion.154
  261.5 1.1 constant_dynamic-update-slice_fusion.155
  262.6 1.0 constant_dynamic-update-slice_fusion.156
  268.2 2.1 constant_dynamic-slice_fusion.41
  307.9 1.2 constant_dynamic-update-slice_fusion.150
  310.7 1.0 constant_dynamic-update-slice_fusion.153
  311.7 1.0 constant_dynamic-update-slice_fusion.154
  312.7 1.1 constant_dynamic-update-slice_fusion.155
  313.9 1.0 constant_dynamic-update-slice_fusion.156
  319.5 2.1 constant_dynamic-slice_fusion.41
  359.2 1.2 constant_dynamic-update-slice_fusion.150
  361.9 1.0 constant_dynamic-update-slice_fusion.153
  362.9 1.0 constant_dynamic-update-slice_fusion.154
  364.0 1.1 constant_dynamic-update-slice_fusion.155
  365.1 1.0 constant_dynamic-update-slice_fusion.156
  370.8 2.1 constant_dynamic-slice_fusion.41
  410.4 1.2 constant_dynamic-update-slice_fusion.150
  413.2 1.0 constant_dynamic-update-slice_fusion.153
  414.2 1.0 constant_dynamic-update-slice_fusion.154
  415.3 1.1 constant_dynamic-update-slice_fusion.155
  416.4 1.0 constant_dynamic-update-slice_fusion.156
  422.0 2.1 constant_dynamic-slice_fusion.41
  461.7 1.2 constant_dynamic-update-slice_fusion.150
  464.5 1.0 constant_dynamic-update-slice_fusion.153
  465.5 1.0 constant_dynamic-update-slice_fusion.154
  466.6 1.1 constant_dynamic-update-slice_fusion.155
  467.7 1.0 constant_dynamic-update-slice_fusion.156
  473.3 2.1 constant_dynamic-slice_fusion.41
  513.0 1.2 constant_dynamic-update-slice_fusion.150
  515.8 1.0 constant_dynamic-update-slice_fusion.153
  516.8 1.1 constant_dynamic-update-slice_fusion.154
  517.9 1.1 constant_dynamic-update-slice_fusion.155
  519.0 1.0 constant_dynamic-update-slice_fusion.156
  524.6 2.1 constant_dynamic-slice_fusion.41
  564.3 1.2 constant_dynamic-update-slice_fusion.150
  567.1 1.0 constant_dynamic-update-slice_fusion.153
  568.1 1.0 constant_dynamic-update-slice_fusion.154
  569.1 1.1 constant_dynamic-update-slice_fusion.155
  570.3 1.1 constant_dynamic-update-slice_fusion.156
  575.9 2.1 constant_dynamic-slice_fusion.41
  611.3 40.9 %copy.111 = bf16[2,512,8192]{1,0,2:T(2,128)(2,1)} copy(bf16[2,512,8192]{2,1,0:T(8,128)(2,1)} %get-tuple-element.323) | data formatting | bytes 33554432 | tf_op jit(solution)/shard_map/while | solution.py:92
  652.2 368.3 %all_to_all.18 = bf16[2,512,8192]{1,0,2:T(2,128)(2,1)} all-to-all(bf16[2,512,8192]{1,0,2:T(2,128)(2,1)} %copy.111), channel_id=1, replica_groups=mesh['freq'=2,'src'=16] {'src'}, dimensions={2} | all-to-all | bytes 33554432 | tf_op jit(solution)/shard_map/all_to_all | solution.py:95
  1020.5 40.8 %copy.112 = bf16[2,16,512,512]{3,2,1,0:T(8,128)(2,1)} copy(bf16[2,16,512,512]{2,0,3,1:T(2,128)(2,1)} %bitcast.624) | data formatting | bytes 33554432 | tf_op jit(solution)/shard_map/all_to_all | solution.py:95
  (1433 shorter events, 346.9 us)
Async XLA Ops:
  6.5 188.4 %all-gather.3.cloned.1.call-start = ((), (), s32[]{:S(2)}) async-start(), calls=%async_computation.1 | async-start | bytes 22282240 | tf_op jit(solution)/shard_map/all_gather | solution.py:62
  78.3 5.8 copy-start
  206.5 4.7 copy-start.13
  206.5 4.7 copy-start.15
  206.5 4.7 copy-start.37
  206.6 4.7 copy-start.39
  210.2 5.3 copy-start.35
  212.4 3.8 copy-start.1
  212.4 3.8 copy-start.3
  212.4 3.8 copy-start.5
  257.8 4.7 copy-start.13
  257.8 4.7 copy-start.15
  257.8 4.7 copy-start.37
  257.8 4.7 copy-start.39
  261.4 5.3 copy-start.35
  263.6 3.8 copy-start.1
  263.6 3.8 copy-start.3
  263.6 3.8 copy-start.5
  309.1 4.7 copy-start.13
  309.1 4.7 copy-start.15
  309.1 4.7 copy-start.37
  309.1 4.7 copy-start.39
  312.7 5.3 copy-start.35
  314.9 3.8 copy-start.1
  314.9 3.8 copy-start.3
  314.9 3.8 copy-start.5
  360.4 4.7 copy-start.13
  360.4 4.7 copy-start.15
  360.4 4.7 copy-start.37
  360.4 4.7 copy-start.39
  364.0 5.3 copy-start.35
  366.2 3.8 copy-start.1
  366.2 3.8 copy-start.3
  366.2 3.8 copy-start.5
  411.6 4.7 copy-start.13
  411.6 4.7 copy-start.15
  411.6 4.7 copy-start.37
  411.7 4.7 copy-start.39
  415.3 5.3 copy-start.35
  417.5 3.8 copy-start.1
  417.5 3.8 copy-start.3
  417.5 3.8 copy-start.5
  462.9 4.7 copy-start.13
  462.9 4.7 copy-start.15
  462.9 4.7 copy-start.37
  463.0 4.7 copy-start.39
  466.6 5.3 copy-start.35
  468.7 3.8 copy-start.1
  468.8 3.8 copy-start.3
  514.2 4.8 copy-start.13
  514.2 4.8 copy-start.15
  514.2 4.8 copy-start.37
  514.2 4.8 copy-start.39
  517.9 5.3 copy-start.35
  520.0 3.8 copy-start.1
  520.0 3.8 copy-start.3
  520.1 3.8 copy-start.5
  565.5 4.7 copy-start.13
  565.5 4.7 copy-start.15
  565.5 4.7 copy-start.37
  565.5 4.7 copy-start.39
  569.1 5.3 copy-start.35
  571.3 3.8 copy-start.1
  571.3 3.8 copy-start.3
  (259 other events, 438.6 us)
Sparse Core Ops, SparseCore 0:
  88.9 106.0 all-gather.2
where the time goes:
time: 1080 us; the launch traced here: 1070 us
  blocking collectives  392 us (36%)
  local copies, waits for them, and re-layouts  367 us (34%)
  other arithmetic  149 us (14%)
  waiting for transfers between devices  105 us (10%)
  matrix products  34.8 us (3%)
  between operations  13.7 us (1%)
    all_to_all x1, blocking collectives, per_device(): lax.all_to_all(rows_result, 'src', split_axis=2, concat_axis=1, tiled=True)  368 us
    while x792, local copies, waits for them, and re-layouts  145 us
    all_gather x1, waiting for transfers between devices, per_device(): band_all = lax.all_gather(band_local, 'src', axis=0, tiled=True)  105 us
    dynamic_update_slice x64, other arithmetic, one_group(): lax.dynamic_update_slice(output, column, (jnp.int32(0), jnp.int32(0), j *...  48 us
    neg x64, other arithmetic, block_column(): -right_im  47.3 us
    while x2, local copies, waits for them, and re-layouts, per_device(): lax.fori_loop(0, block_count // 8, one_group, jnp.zeros((2, row_count, bl...  41 us
    all_to_all x1, local copies, waits for them, and re-layouts, per_device(): lax.all_to_all(rows_result, 'src', split_axis=2, concat_axis=1, tiled=True)  40.8 us
    mul x64, other arithmetic, block_column(): left_all = left_all * mask_col.astype(jnp.bfloat16)[None, :, None, :, None]  39.8 us
  transfers between devices with their start and end apart: 1, of which 1 were waited for; matrix products, arithmetic and copies ran while one was open for 0% of the time, Pallas kernels for 0%

commit v1 on v0

v1 whole, which is shorter than its diff:
```python
import functools

import jax
import jax.numpy as jnp
from jax import lax
from jax.experimental import pallas as pl
from jax.experimental.pallas import tpu as pltpu
from jax.sharding import PartitionSpec as P

BLK = 128
APW = 2
WIN = 2 * APW + 1
HALO = APW * BLK
SMALL_ROWS = 8


def xor_index(index, d):
    bit, result = 1, index
    while bit <= d:
        if d & bit:
            result = result + bit - 2 * bit * ((index // bit) % 2)
        bit *= 2
    return result


def exchange_kernel(n, rows, width, shots, small, recv, small_all,
                    base_s, base_r, mate_s, mate_r, ext_s, ext_r, sm_s, sm_r, loc):
    me = lax.axis_index("src")
    half = n // 2
    odd = me % 2
    mate = xor_index(me, 1)

    def edge(t):
        return (t == 0) | (t == n - 1)

    def middle(t):
        return (t == half - 1) | (t == half)

    def rows_of(s, col, wide):
        return recv.at[:, pl.ds(pl.multiple_of(s * rows, rows), rows), pl.ds(pl.multiple_of(col, BLK), wide)]

    def cols_of(col, wide):
        return shots.at[:, :, pl.ds(pl.multiple_of(col, BLK), wide)]

    def remote(src, dst, send, got, t):
        return pltpu.make_async_remote_copy(
            src_ref=src, dst_ref=dst, send_sem=send, recv_sem=got,
            device_id={"src": t}, device_id_type=pl.DeviceIdType.MESH)

    def span(t, wide_case, both):
        t_odd = t % 2
        if both:
            if wide_case:
                return t * width - HALO, 0, width + 2 * HALO
            return t * width - HALO * t_odd, HALO * (1 - t_odd), width + HALO
        if wide_case:
            return t * width - HALO * (1 - t_odd), HALO * t_odd, width + HALO
        return t * width, HALO, width

    def wide_for(t, d):
        if d < half:
            return jnp.logical_not(edge(t))
        return middle(t)

    def both_ways(cond, act):
        @pl.when(cond)
        def _():
            act(True)

        @pl.when(jnp.logical_not(cond))
        def _():
            act(False)

    def outgoing(d, wide_case):
        t = xor_index(me, d)
        src_col, dst_col, wide = span(t, wide_case, d <= 1)
        return remote(cols_of(src_col, wide), rows_of(me, dst_col, wide), base_s.at[d], base_r.at[d], t)

    def incoming(d, wide_case):
        s = xor_index(me, d)
        _, dst_col, wide = span(me, wide_case, d <= 1)
        place = rows_of(s, dst_col, wide)
        return remote(place, place, base_s.at[d], base_r.at[d], s)

    def own_copy(wide_case):
        src_col, dst_col, wide = span(me, wide_case, True)
        return pltpu.make_async_copy(cols_of(src_col, wide), rows_of(me, dst_col, wide), loc.at[0])

    def mate_out(d):
        s = xor_index(me, d)
        src = rows_of(s, width * (1 - odd) + HALO * odd, HALO)
        return remote(src, rows_of(s, (HALO + width) * odd, HALO), mate_s.at[d], mate_r.at[d], mate)

    def mate_in(d):
        place = rows_of(xor_index(mate, d), (HALO + width) * (1 - odd), HALO)
        return remote(place, place, mate_s.at[d], mate_r.at[d], mate)

    neighbour = me - 1 + 2 * odd
    hands_on = jnp.logical_not(edge(me) | middle(me))

    def ext_out(d):
        s = xor_index(me, d)
        src = rows_of(s, HALO * (1 - odd) + width * odd, HALO)
        return remote(src, rows_of(s, (HALO + width) * (1 - odd), HALO), ext_s.at[d], ext_r.at[d], neighbour)

    def ext_in(d):
        place = rows_of(xor_index(neighbour, d), (HALO + width) * odd, HALO)
        return remote(place, place, ext_s.at[d], ext_r.at[d], neighbour)

    def small_out(d):
        return remote(small, small_all.at[me], sm_s.at[d], sm_r.at[d], xor_index(me, d))

    def small_in(d):
        place = small_all.at[xor_index(me, d)]
        return remote(place, place, sm_s.at[d], sm_r.at[d], xor_index(me, d))

    barrier = pltpu.get_barrier_semaphore()
    for d in range(1, n):
        pl.semaphore_signal(barrier, inc=1, device_id={"src": xor_index(me, d)},
                            device_id_type=pl.DeviceIdType.MESH)
    pl.semaphore_wait(barrier, n - 1)

    far = list(range(n - 1, half - 1, -1))
    near = list(range(half - 1, 0, -1))
    order = [far[0]]
    for f, g in zip(far[1:], near):
        order += [g, f]

    for d in order:
        both_ways(wide_for(xor_index(me, d), d), lambda w, d=d: outgoing(d, w).start())
    both_ways(jnp.logical_not(edge(me)), lambda w: own_copy(w).start())
    small_own = pltpu.make_async_copy(small, small_all.at[me], loc.at[1])
    small_own.start()
    for d in range(1, n):
        small_out(d).start()

    for d in order:
        both_ways(wide_for(me, d), lambda w, d=d: incoming(d, w).wait_recv())
        if d > 1:
            mate_out(d).start()
        if d >= half:
            @pl.when(hands_on)
            def _(d=d):
                ext_out(d).start()

    for d in order:
        both_ways(wide_for(xor_index(me, d), d), lambda w, d=d: outgoing(d, w).wait_send())
        small_out(d).wait_send()
        small_in(d).wait_recv()
        if d > 1:
            mate_out(d).wait_send()
            mate_in(d).wait_recv()
        if d >= half:
            @pl.when(hands_on)
            def _(d=d):
                ext_out(d).wait_send()
                ext_in(d).wait_recv()
    both_ways(jnp.logical_not(edge(me)), lambda w: own_copy(w).wait())
    small_own.wait()


def product_kernel(rows, width, block_total, me_ref, aper, small, obl, recv, *rest):
    bands, out, rhs, left = rest[:-3], rest[-3], rest[-2], rest[-1]
    step = pl.program_id(0)
    me = me_ref[0]
    cols = width // BLK
    row_blocks = rows // BLK

    def make_data(block_ref, wave, start, wide):
        wave_re, wave_im = wave[:, 0:1], wave[:, 1:2]
        re = block_ref[0, :, start:start + wide].astype(jnp.float32)
        im = block_ref[1, :, start:start + wide].astype(jnp.float32)
        factor = obl[0:1, start:start + wide]
        s_re = (re * wave_re - im * wave_im).astype(jnp.bfloat16).astype(jnp.float32)
        s_im = (re * wave_im + im * wave_re).astype(jnp.bfloat16).astype(jnp.float32)
        return (s_re * factor).astype(jnp.bfloat16), (s_im * factor).astype(jnp.bfloat16)

    @pl.when(step == 0)
    def _():
        per = rows // HALO
        total = (block_total * BLK) // HALO
        for b, band in enumerate(bands):
            g = jnp.clip(me * (width // HALO) - 1 + b, 0, total - 1)
            lanes = pl.ds(pl.multiple_of((g % per) * HALO, BLK), HALO)
            wave = jnp.transpose(small[g // per, :, lanes])
            for j in range(cols):
                pair = [k for k in (APW * b, APW * b + 1) if 0 <= k - j < WIN]
                if not pair:
                    continue
                b_re, b_im = make_data(band, wave, HALO + j * BLK, BLK)
                for k in pair:
                    part = slice((k - APW * b) * BLK, (k - APW * b + 1) * BLK)
                    top = (k - j) * 2 * BLK
                    rhs[j, top:top + BLK, :BLK] = -b_re[part]
                    rhs[j, top:top + BLK, BLK:] = -b_im[part]
                    rhs[j, top + BLK:top + 2 * BLK, :BLK] = b_im[part]
                    rhs[j, top + BLK:top + 2 * BLK, BLK:] = -b_re[part]

    wave = jnp.transpose(small[step])
    for k in range(cols + 2 * APW):
        d_re, d_im = make_data(recv, wave, k * BLK, BLK)
        left[:, 2 * k * BLK:(2 * k + 1) * BLK] = d_re
        left[:, (2 * k + 1) * BLK:(2 * k + 2) * BLK] = d_im

    for j in range(cols):
        strips = []
        for r in range(row_blocks):
            listed = [aper[step * row_blocks + r, j * aper.shape[1] // cols + t] for t in range(aper.shape[1] // cols)]
            pieces = []
            for w in range(WIN):
                k = me * cols + j + w - APW
                hit = listed[0] == k
                for entry in listed[1:]:
                    hit = hit | (entry == k)
                hit = hit & (k >= 0) & (k < block_total)
                piece = left[r * BLK:(r + 1) * BLK, (j + w) * 2 * BLK:(j + w + 1) * 2 * BLK]
                pieces.append(jnp.where(hit, piece, jnp.zeros_like(piece)))
            strips.append(jnp.concatenate(pieces, axis=1))
        product = jnp.dot(jnp.concatenate(strips, axis=0), rhs[j], preferred_element_type=jnp.float32)
        out[0, :, j * BLK:(j + 1) * BLK] = product[:, :BLK].astype(jnp.bfloat16)
        out[1, :, j * BLK:(j + 1) * BLK] = product[:, BLK:].astype(jnp.bfloat16)


def per_device(n, shots, wavelet, obliquity, aperture):
    rows, total = shots.shape[1], shots.shape[2]
    width = total // n
    block_total = total // BLK
    row_blocks, _, entries = aperture.shape
    cols = width // BLK
    spread = width + 2 * HALO
    me = lax.axis_index("src")
    aper_rows = row_blocks * block_total * entries // rows
    small = jnp.concatenate([
        wavelet,
        obliquity[None, :],
        aperture.astype(jnp.float32).reshape(aper_rows, rows),
        jnp.zeros((SMALL_ROWS - 3 - aper_rows, rows), jnp.float32),
    ])
    anywhere = pl.BlockSpec(memory_space=pl.ANY)
    recv, small_all = pl.pallas_call(
        functools.partial(exchange_kernel, n, rows, width),
        out_shape=(
            jax.ShapeDtypeStruct((2, total, spread), shots.dtype),
            jax.ShapeDtypeStruct((n, SMALL_ROWS, rows), jnp.float32),
        ),
        in_specs=[anywhere, anywhere],
        out_specs=(anywhere, anywhere),
        scratch_shapes=[pltpu.SemaphoreType.DMA((n,))] * 8 + [pltpu.SemaphoreType.DMA((2,))],
        compiler_params=pltpu.CompilerParams(collective_id=0, has_side_effects=True),
    )(shots, small)

    aper = small_all[:, 3:3 + aper_rows].astype(jnp.int32).reshape(block_total, block_total * entries)
    aper = lax.dynamic_slice(aper, (jnp.int32(0), me * cols * entries), (block_total, cols * entries))
    before = lax.dynamic_slice(small_all, (jnp.maximum(me - 1, 0), 2, rows - HALO), (1, 1, HALO))
    after = lax.dynamic_slice(small_all, (jnp.minimum(me + 1, n - 1), 2, 0), (1, 1, HALO))
    obl = jnp.concatenate([before[0, 0], obliquity, after[0, 0]])[None, :]

    band_count = width // HALO + 2
    band_total = total // HALO


    return pl.pallas_call(
        functools.partial(product_kernel, rows, width, block_total),
        grid_spec=pltpu.PrefetchScalarGridSpec(
            num_scalar_prefetch=2,
            grid=(n,),
            in_specs=[
                pl.BlockSpec((n, SMALL_ROWS, rows), lambda i, *_: (0, 0, 0)),
                pl.BlockSpec((1, spread), lambda i, *_: (0, 0)),
                pl.BlockSpec((2, rows, spread), lambda i, *_: (0, i, 0)),
            ] + [
                pl.BlockSpec(
                    (2, HALO, spread),
                    lambda i, me_ref, aper_ref, b=b: (
                        0, jnp.clip(me_ref[0] * (width // HALO) - 1 + b, 0, band_total - 1), 0))
                for b in range(band_count)
            ],
            out_specs=pl.BlockSpec((2, rows, width), lambda i, *_: (0, i, 0)),
            scratch_shapes=[
                pltpu.VMEM((cols, WIN * 2 * BLK, 2 * BLK), jnp.bfloat16),
                pltpu.VMEM((rows, (cols + 2 * APW) * 2 * BLK), jnp.bfloat16),
            ],
        ),
        out_shape=jax.ShapeDtypeStruct((2, total, width), jnp.bfloat16),
        compiler_params=pltpu.CompilerParams(vmem_limit_bytes=48 * 1024 * 1024),
    )(me[None], aper, small_all, obl, recv, *([recv] * band_count))


def solution(mesh):
    return jax.shard_map(
        functools.partial(per_device, mesh.shape["src"]),
        mesh=mesh,
        in_specs=(P("freq", "src", None), P("freq", "src"), P("src"), P("src", None, None)),
        out_specs=P("freq", None, "src"),
        check_vma=False,
    )
```

time: 1080 us -> 503 us (0.47); the launches traced: 1070 us -> 502 us
  Pallas kernels: 0 us -> 497 us
  blocking collectives: 392 us -> 0 us
  local copies, waits for them, and re-layouts: 367 us -> 2.14 us
  other arithmetic: 149 us -> 3.08 us
  waiting for transfers between devices: 105 us -> 0 us
  matrix products: 34.8 us -> 0 us
  between operations: 13.7 us -> 0.03 us
    pallas_call x0 -> x2, Pallas kernels: none -> 497 us  [the longest x1 456 us: per_device(): pl.pallas_call(functools.partial(exchange_kernel, n, rows, width), out_sh...]
    all_to_all x1 -> x0, blocking collectives: 368 us -> none  [per_device(): lax.all_to_all(rows_result, 'src', split_axis=2, concat_axis=1, tiled=True)]
    while x794 -> x0, local copies, waits for them, and re-layouts: 186 us -> none
    all_gather x1 -> x0, waiting for transfers between devices: 105 us -> none  [per_device(): band_all = lax.all_gather(band_local, 'src', axis=0, tiled=True)]
    dynamic_update_slice x64 -> x0, other arithmetic: 48 us -> none  [one_group(): lax.dynamic_update_slice(output, column, (jnp.int32(0), jnp.int32(0), j *...]
    neg x64 -> x0, other arithmetic: 47.3 us -> none  [block_column(): -right_im]
    slice x66 -> x0, local copies, waits for them, and re-layouts: 45.8 us -> none  [the longest x64 33.3 us: block_column(): left_big = jnp.concatenate([left_all[0], left_all[1]], axis=1)]
    all_to_all x1 -> x0, local copies, waits for them, and re-layouts: 40.8 us -> none  [per_device(): lax.all_to_all(rows_result, 'src', split_axis=2, concat_axis=1, tiled=True)]
  transfers between devices with their start and end apart: 1 -> 0, of which waited for: 1 -> 0; matrix products, arithmetic and copies ran while one was open for 0% -> 0% of each run, Pallas kernels for 0% -> 0%
where the time goes in v1:
time: 503 us; the launch traced here: 502 us
  Pallas kernels  497 us (99%)
    pallas_call x1, Pallas kernels, per_device(): pl.pallas_call(functools.partial(exchange_kernel, n, rows, width), out_sh...  456 us
    pallas_call x1, Pallas kernels, per_device(): pl.pallas_call(functools.partial(product_kernel, rows, width, block_total...  41.3 us

profile of v1, /device:TPU:1, one launch (start us, length us, event | category | flops | bytes accessed | tf_op | source)
XLA Modules:
  0.0 502.2 jit_solution(6200893696624714354)
XLA Ops:
  0.0 0.0 copy-start.1
  0.0 0.1 pad.6.clone
  0.1 0.7 convert_element_type.6
  0.8 0.1 copy.6
  0.9 0.1 reshape.6
  1.0 1.4 maximum_maximum_fusion.small
  2.4 455.7 %shard_map.46 = (bf16[2,8192,1024]{2,1,0:T(8,128)(2,1)}, f32[16,8,512]{2,1,0:T(8,128)}) custom-call(bf16[2,512,8192]{2,1,0:T(8,128)(2,1)} %shots.1, f32[8,512]{1,0:T(8,128)} %maximum_maximum_fusion.small), custom_call_target="tpu_custom_call" | custom-call | tf_op jit(solution)/shard_map/pallas_call | solution.py:240
  458.1 0.7 constant_dynamic-slice_fusion.1
  458.9 0.0 copy-done.1
  458.9 1.0 slice_convert_fusion
  459.9 0.1 reshape.7
  459.9 0.1 constant_dynamic-slice_fusion.2.aper
  460.0 0.0 copy-start
  460.0 1.0 copy-done
  461.0 41.3 %shard_map.47 = bf16[2,8192,512]{2,1,0:T(8,128)(2,1)} custom-call(s32[1]{0:T(128)} %bitcast.me_ref, s32[64,16]{1,0:T(8,128)S(1)} %constant_dynamic-slice_fusion.2.aper, f32[16,8,512]{2,1,0:T(8,128)S(1)} %copy-done, f32[1,1024]{1,0:T(1,128)S(1)} %bitcast.5, bf16[2,8192,1024]{2,1,0:T(8,128)(2,1)} %get-tuple-element.8.recv.rest_0_.rest_1_.rest_2_.rest_3_, ...), custom_call_target="tpu_custom_call" | custom-call | tf_op jit(solution)/shard_map/pallas_call | solution.py:262
  (2 shorter events, 0.0 us)
Async XLA Ops:
  0.0 458.9 %copy-start.1 = (f32[512]{0:T(512)S(1)}, f32[512]{0:T(512)}, u32[]{:S(2)}) copy-start(f32[512]{0:T(512)} %param.6) | copy-start | bytes 6148
  460.0 1.0 copy-start

commit v2 on v1

--- a/solution.py
+++ b/solution.py
@@ -12,6 +12,7 @@
 WIN = 2 * APW + 1
 HALO = APW * BLK
 SMALL_ROWS = 8
+AHEAD = 3
 
 
 def xor_index(index, d):
@@ -122,29 +123,41 @@
 
     far = list(range(n - 1, half - 1, -1))
     near = list(range(half - 1, 0, -1))
-    order = [far[0]]
-    for f, g in zip(far[1:], near):
-        order += [g, f]
-
-    for d in order:
-        both_ways(wide_for(xor_index(me, d), d), lambda w, d=d: outgoing(d, w).start())
+
+    def sends(is_odd):
+        return near + far if is_odd else far + near
+
+    def arrivals(is_odd):
+        place = {d: sends(bool(is_odd) != bool(d % 2)).index(d) for d in far + near}
+        return sorted(far + near, key=lambda d: place[d])
+
     both_ways(jnp.logical_not(edge(me)), lambda w: own_copy(w).start())
     small_own = pltpu.make_async_copy(small, small_all.at[me], loc.at[1])
     small_own.start()
     for d in range(1, n):
         small_out(d).start()
 
-    for d in order:
-        both_ways(wide_for(me, d), lambda w, d=d: incoming(d, w).wait_recv())
-        if d > 1:
-            mate_out(d).start()
-        if d >= half:
-            @pl.when(hands_on)
-            def _(d=d):
-                ext_out(d).start()
-
-    for d in order:
-        both_ways(wide_for(xor_index(me, d), d), lambda w, d=d: outgoing(d, w).wait_send())
+    def run(is_odd):
+        todo, come = sends(is_odd), arrivals(is_odd)
+        for i in range(n - 1 + AHEAD):
+            if i < n - 1:
+                d = todo[i]
+                both_ways(wide_for(xor_index(me, d), d), lambda w, d=d: outgoing(d, w).start())
+            if i >= AHEAD:
+                d = todo[i - AHEAD]
+                both_ways(wide_for(xor_index(me, d), d), lambda w, d=d: outgoing(d, w).wait_send())
+                d = come[i - AHEAD]
+                both_ways(wide_for(me, d), lambda w, d=d: incoming(d, w).wait_recv())
+                if d >= half:
+                    @pl.when(hands_on)
+                    def _(d=d):
+                        ext_out(d).start()
+                if d > 1:
+                    mate_out(d).start()
+
+    both_ways(odd == 1, run)
+
+    for d in range(1, n):
         small_out(d).wait_send()
         small_in(d).wait_recv()
         if d > 1:

time: 503 us -> 450 us (0.89)
  Pallas kernels: 497 us -> 444 us
    pallas_call x1, Pallas kernels: 456 us -> 403 us  [per_device(): pl.pallas_call(functools.partial(exchange_kernel, n, rows, width), out_sh...]
where the time goes in v2:
time: 450 us; the launch traced here: 449 us
  Pallas kernels  444 us (99%)
    pallas_call x1, Pallas kernels, per_device(): pl.pallas_call(functools.partial(exchange_kernel, n, rows, width), out_sh...  403 us
    pallas_call x1, Pallas kernels, per_device(): pl.pallas_call(functools.partial(product_kernel, rows, width, block_total...  41.3 us

profile of v2, /device:TPU:1, one launch (start us, length us, event | category | flops | bytes accessed | tf_op | source)
XLA Modules:
  0.0 449.4 jit_solution(13660439981505292429)
XLA Ops:
  0.0 0.0 copy-start.1
  0.0 0.1 pad.6.clone
  0.1 0.7 convert_element_type.6
  0.8 0.1 copy.6
  0.9 0.1 reshape.6
  1.0 1.4 maximum_maximum_fusion.small
  2.4 402.8 %shard_map.46 = (bf16[2,8192,1024]{2,1,0:T(8,128)(2,1)}, f32[16,8,512]{2,1,0:T(8,128)}) custom-call(bf16[2,512,8192]{2,1,0:T(8,128)(2,1)} %shots.1, f32[8,512]{1,0:T(8,128)} %maximum_maximum_fusion.small), custom_call_target="tpu_custom_call" | custom-call | tf_op jit(solution)/shard_map/pallas_call | solution.py:253
  405.3 0.7 constant_dynamic-slice_fusion.1
  406.0 0.0 copy-done.1
  406.0 1.0 slice_convert_fusion
  407.0 0.1 reshape.7
  407.1 0.1 constant_dynamic-slice_fusion.2.aper
  407.1 0.0 copy-start
  407.1 1.0 copy-done
  408.1 41.3 %shard_map.47 = bf16[2,8192,512]{2,1,0:T(8,128)(2,1)} custom-call(s32[1]{0:T(128)} %bitcast.me_ref, s32[64,16]{1,0:T(8,128)S(1)} %constant_dynamic-slice_fusion.2.aper, f32[16,8,512]{2,1,0:T(8,128)S(1)} %copy-done, f32[1,1024]{1,0:T(1,128)S(1)} %bitcast.5, bf16[2,8192,1024]{2,1,0:T(8,128)(2,1)} %get-tuple-element.8.recv.rest_0_.rest_1_.rest_2_.rest_3_, ...), custom_call_target="tpu_custom_call" | custom-call | tf_op jit(solution)/shard_map/pallas_call | solution.py:275
  (2 shorter events, 0.0 us)
Async XLA Ops:
  0.0 406.0 %copy-start.1 = (f32[512]{0:T(512)S(1)}, f32[512]{0:T(512)}, u32[]{:S(2)}) copy-start(f32[512]{0:T(512)} %param.6) | copy-start | bytes 6148
  407.1 1.0 copy-start
